TPU v7x, 512 devices: a whole 4x8x8 slice. The times are simulated.
512 devices in a mesh: seq: 64 (over z_hi, x, y), tp: 8 (over z_lo, core).
Axes of the slice: x: 4, y: 8, z: 8 (z_hi: 2, z_lo: 4; z = z_hi * 4 + z_lo), core: 2. Of those that a mesh axis runs over, the one named last changes fastest.
Arguments:
- features: bfloat16 [8192, 8192], P('seq', 'tp'), may hold values from -6 to 6
- in_proj: bfloat16 [3, 8192, 1024], P(None, 'seq', 'tp'), may hold values from -0.0625 to 0.0625
- short_taps: float32 [3, 3, 1024], P(None, None, 'tp'), may hold values from -3 to 3
- long_filter: float32 [8192, 1024], P('seq', 'tp'), may hold values from -1.8 to 1.8
- skip_gain: float32 [1024], P('tp'), may hold values from -4 to 4
- out_proj: bfloat16 [1024, 8192], P('tp', 'seq'), may hold values from -0.1875 to 0.1875
Outputs:
- mixed: bfloat16 [8192, 8192], P('seq', 'tp')
All inputs are finite; a program needn't handle non-finite values.
Results may differ from a plain program's by a relative error of at most 0.007.
Values may be sent and summed in bfloat16 or wider, within the bound.
A program may use at most 64 MiB of HBM per device.

v0:
```python
import math
import jax
import jax.numpy as jnp
from jax import lax
from jax.sharding import PartitionSpec as P

HIGHEST = lax.Precision.HIGHEST


def from_behind(array, axis, by):
    count = lax.axis_size(axis)
    pairs = [(i, i + by) for i in range(count) if 0 <= i + by < count]
    return lax.ppermute(array, axis, pairs)


def contract(form, table, values):
    return jnp.einsum(form, table, values, precision=HIGHEST, preferred_element_type=jnp.float32)


def complex_apply(form, tab_real, tab_imag, in_real, in_imag):
    out_real = contract(form, tab_real, in_real) - contract(form, tab_imag, in_imag)
    out_imag = contract(form, tab_real, in_imag) + contract(form, tab_imag, in_real)
    return (out_real, out_imag)


def phases(first, second, modulus, sign):
    product = first[:, None] * second[None, :] % modulus
    angle = sign * 2.0 * math.pi / modulus * product.astype(jnp.float32)
    return (jnp.cos(angle), jnp.sin(angle))


def split_factor(total):
    first_len = 1
    for cand in range(1, total + 1):
        if cand * cand > total:
            break
        if total % cand == 0:
            first_len = cand
    return (first_len, total // first_len)


def local_forward(in_real, in_imag):
    count, tok_rows, chan_dev = in_real.shape
    first_len, second_len = split_factor(tok_rows)
    in_real = in_real.reshape(count, first_len, second_len, chan_dev)
    in_imag = in_imag.reshape(count, first_len, second_len, chan_dev)
    index_first = jnp.arange(first_len, dtype=jnp.int32)
    index_second = jnp.arange(second_len, dtype=jnp.int32)
    tab_real, tab_imag = phases(index_first, index_first, first_len, -1.0)
    mid_real, mid_imag = complex_apply("ma,qabc->qmbc", tab_real, tab_imag, in_real, in_imag)
    turn_real, turn_imag = phases(index_first, index_second, tok_rows, -1.0)
    turn_real = turn_real[None, :, :, None]
    turn_imag = turn_imag[None, :, :, None]
    mid_real, mid_imag = (
        mid_real * turn_real - mid_imag * turn_imag,
        mid_real * turn_imag + mid_imag * turn_real,
    )
    tab_real, tab_imag = phases(index_second, index_second, second_len, -1.0)
    out_real, out_imag = complex_apply("nb,qmbc->qmnc", tab_real, tab_imag, mid_real, mid_imag)
    return (
        out_real.reshape(count, tok_rows, chan_dev),
        out_imag.reshape(count, tok_rows, chan_dev),
    )


def local_inverse(in_real, in_imag):
    count, tok_rows, chan_dev = in_real.shape
    first_len, second_len = split_factor(tok_rows)
    in_real = in_real.reshape(count, first_len, second_len, chan_dev)
    in_imag = in_imag.reshape(count, first_len, second_len, chan_dev)
    index_first = jnp.arange(first_len, dtype=jnp.int32)
    index_second = jnp.arange(second_len, dtype=jnp.int32)
    tab_real, tab_imag = phases(index_second, index_second, second_len, 1.0)
    mid_real, mid_imag = complex_apply("bn,qmnc->qmbc", tab_real, tab_imag, in_real, in_imag)
    turn_real, turn_imag = phases(index_first, index_second, tok_rows, 1.0)
    turn_real = turn_real[None, :, :, None]
    turn_imag = turn_imag[None, :, :, None]
    mid_real, mid_imag = (
        mid_real * turn_real - mid_imag * turn_imag,
        mid_real * turn_imag + mid_imag * turn_real,
    )
    tab_real, tab_imag = phases(index_first, index_first, first_len, 1.0)
    out_real, out_imag = complex_apply("am,qmbc->qabc", tab_real, tab_imag, mid_real, mid_imag)
    return (
        out_real.reshape(count, tok_rows, chan_dev),
        out_imag.reshape(count, tok_rows, chan_dev),
    )


def long_convolve(inner, long_filter):
    tok_rows, chan_dev = inner.shape
    seq_parts = lax.axis_size("seq")
    position = lax.axis_index("seq")
    seq_rows = tok_rows // seq_parts
    freq_count = 2 * seq_parts
    pad_length = 2 * tok_rows * seq_parts
    sent_inner, sent_filter = (
        lax.all_to_all(inner[None], "seq", split_axis=1, concat_axis=0, tiled=True),
        lax.all_to_all(long_filter[None], "seq", split_axis=1, concat_axis=0, tiled=True),
    )
    freq_index = jnp.arange(freq_count, dtype=jnp.int32)
    block_index = jnp.arange(seq_parts, dtype=jnp.int32)
    tab_real, tab_imag = phases(freq_index, block_index, freq_count, -1.0)
    inner_real = contract("qp,prc->qrc", tab_real, sent_inner)
    inner_imag = contract("qp,prc->qrc", tab_imag, sent_inner)
    filter_real = contract("qp,prc->qrc", tab_real, sent_filter)
    filter_imag = contract("qp,prc->qrc", tab_imag, sent_filter)
    global_rows = position * seq_rows + jnp.arange(seq_rows, dtype=jnp.int32)
    turn_real, turn_imag = phases(freq_index, global_rows, pad_length, -1.0)
    turn_real = turn_real[:, :, None]
    turn_imag = turn_imag[:, :, None]
    inner_real, inner_imag = (
        inner_real * turn_real - inner_imag * turn_imag,
        inner_real * turn_imag + inner_imag * turn_real,
    )
    filter_real, filter_imag = (
        filter_real * turn_real - filter_imag * turn_imag,
        filter_real * turn_imag + filter_imag * turn_real,
    )
    inner_real, inner_imag, filter_real, filter_imag = (
        lax.all_to_all(inner_real, "seq", split_axis=0, concat_axis=1, tiled=True),
        lax.all_to_all(inner_imag, "seq", split_axis=0, concat_axis=1, tiled=True),
        lax.all_to_all(filter_real, "seq", split_axis=0, concat_axis=1, tiled=True),
        lax.all_to_all(filter_imag, "seq", split_axis=0, concat_axis=1, tiled=True),
    )
    spec_real, spec_imag = local_forward(
        jnp.concatenate([inner_real, filter_real], 0), jnp.concatenate([inner_imag, filter_imag], 0)
    )
    pair = inner_real.shape[0]
    left_real, right_real = (spec_real[:pair], spec_real[pair:])
    left_imag, right_imag = (spec_imag[:pair], spec_imag[pair:])
    prod_real = left_real * right_real - left_imag * right_imag
    prod_imag = left_real * right_imag + left_imag * right_real
    back_real, back_imag = local_inverse(prod_real, prod_imag)
    back_real, back_imag = (
        lax.all_to_all(back_real, "seq", split_axis=1, concat_axis=0, tiled=True),
        lax.all_to_all(back_imag, "seq", split_axis=1, concat_axis=0, tiled=True),
    )
    back_real, back_imag = (
        back_real * turn_real + back_imag * turn_imag,
        back_imag * turn_real - back_real * turn_imag,
    )
    inv_real, inv_imag = phases(block_index, freq_index, freq_count, 1.0)
    values = (
        contract("pq,qrc->prc", inv_real, back_real) - contract("pq,qrc->prc", inv_imag, back_imag)
    ) / pad_length
    result = lax.all_to_all(values, "seq", split_axis=0, concat_axis=1, tiled=True)
    return result[0]


def per_device(features, in_proj, short_taps, long_filter, skip_gain, out_proj):
    tok_rows = features.shape[0]
    chan_dev = in_proj.shape[2]
    taps_count = short_taps.shape[1]
    full_in = lax.all_gather(in_proj, "seq", axis=1, tiled=True)
    full_out = lax.all_gather(out_proj, "seq", axis=1, tiled=True)
    empty = jnp.zeros((3, tok_rows, chan_dev), jnp.float32)
    piece = jax.tree.map(lambda part: lax.all_gather(part, "tp", axis=1, tiled=True), features)
    weight_rows = lax.slice_in_dim(full_in, 0, piece.shape[1], axis=1)
    projected = (
        empty + jnp.einsum("tk,skc->stc", piece, weight_rows, preferred_element_type=jnp.float32)
    ).astype(jnp.bfloat16)
    earlier = from_behind(projected[:, tok_rows - (taps_count - 1) :, :], "seq", 1)
    padded = jnp.concatenate([earlier, projected], axis=1).astype(jnp.float32)
    filtered = jnp.zeros((3, tok_rows, chan_dev), jnp.float32)
    for offset in range(taps_count):
        begin = taps_count - 1 - offset
        filtered = (
            filtered + short_taps[:, offset, None, :] * padded[:, begin : begin + tok_rows, :]
        )
    query = filtered[0]
    inner = filtered[1] * filtered[2]
    long_mix = long_convolve(inner, long_filter)
    gated = (query * (long_mix + skip_gain[None, :] * inner)).astype(jnp.bfloat16)
    terms = jnp.dot(gated, full_out, preferred_element_type=jnp.float32)
    mixed = lax.psum_scatter(terms, "tp", scatter_dimension=1, tiled=True)
    return mixed.astype(jnp.bfloat16)


def solution(mesh):
    return jax.shard_map(
        per_device,
        mesh=mesh,
        in_specs=(
            P("seq", "tp"),
            P(None, "seq", "tp"),
            P(None, None, "tp"),
            P("seq", "tp"),
            P("tp"),
            P("tp", "seq"),
        ),
        out_specs=P("seq", "tp"),
        check_vma=False,
    )
```

profile of v0, /device:TPU:2, one launch (start us, length us, event | category | flops | bytes accessed | tf_op | source)
XLA Modules:
  0.0 527.9 jit_solution(7247148806284053348)
XLA Ops:
  8.0 19.1 %all-to-all-start.2 = ((f32[1,128,128]{2,0,1:T(1,128)}), f32[1,128,128]{2,0,1:T(1,128)S(1)}, u32[]{:S(2)}, u32[]{:S(2)}) async-start(f32[1,128,128]{2,0,1:T(1,128)} %bitcast.186), calls=%async_computation.2 | async-start | bytes 131072 | tf_op jit(solution)/shard_map/all_to_all | solution.py:99
  27.1 0.8 fusion.242
  28.0 28.7 %all-gather.6.cloned.1.call-done = bf16[128,8192]{1,0:T(8,128)(2,1)} async-done(((bf16[128,1024]{1,0:T(8,128)(2,1)}), bf16[128,8192]{1,0:T(8,128)(2,1)}) %all-gather.6.cloned.1.call-update) | async-done | bytes 2097168 | tf_op jit(solution)/shard_map/all_gather | solution.py:158
  56.6 183.0 %all-gather.4.cloned.1.call-done = bf16[3,8192,128]{2,1,0:T(8,128)(2,1)} async-done(((bf16[3,128,128]{2,1,0:T(8,128)(2,1)}), bf16[3,8192,128]{2,1,0:T(8,128)(2,1)}) %all-gather.4.cloned.1.call-update) | async-done | bytes 6291472 | tf_op jit(solution)/shard_map/all_gather | solution.py:155
  239.6 4.7 fusion.11
  244.3 2.9 collective-permute-start
  247.4 4.5 collective-permute-done
  252.7 7.7 %all-to-all-start = ((f32[1,128,128]{2,0,1:T(1,128)}), f32[1,128,128]{2,0,1:T(1,128)S(1)}, u32[]{:S(2)}, u32[]{:S(2)}) async-start(f32[1,128,128]{2,0,1:T(1,128)} %bitcast.5), calls=%async_computation | async-start | bytes 131072 | tf_op jit(solution)/shard_map/all_to_all | solution.py:98
  260.8 13.2 %all-to-all-done = f32[1,128,128]{2,0,1:T(1,128)S(1)} async-done(((f32[1,128,128]{2,0,1:T(1,128)}), f32[1,128,128]{2,0,1:T(1,128)S(1)}, u32[]{:S(2)}, u32[]{:S(2)}) %all-to-all-start) | async-done | bytes 65568 | tf_op jit(solution)/shard_map/all_to_all | solution.py:98
  275.3 0.8 copy.124
  276.1 5.5 %all-to-all-start.3 = ((f32[128,2,128]{2,1,0:T(2,128)}), f32[128,2,128]{2,1,0:T(2,128)S(1)}, u32[]{:S(2)}, u32[]{:S(2)}) async-start(f32[128,2,128]{2,1,0:T(2,128)} %copy.124), calls=%async_computation.3 | async-start | bytes 262144 | tf_op jit(solution)/shard_map/all_to_all | solution.py:123
  281.6 0.7 copy.130
  282.4 13.2 %all-to-all-done.3 = f32[128,2,128]{2,1,0:T(2,128)S(1)} async-done(((f32[128,2,128]{2,1,0:T(2,128)}), f32[128,2,128]{2,1,0:T(2,128)S(1)}, u32[]{:S(2)}, u32[]{:S(2)}) %all-to-all-start.3) | async-done | bytes 131104 | tf_op jit(solution)/shard_map/all_to_all | solution.py:123
  295.6 5.7 %all-to-all-start.5 = ((f32[128,2,128]{2,1,0:T(2,128)}), f32[128,2,128]{2,1,0:T(2,128)S(1)}, u32[]{:S(2)}, u32[]{:S(2)}) async-start(f32[128,2,128]{2,1,0:T(2,128)} %copy.130), calls=%async_computation.5 | async-start | bytes 262144 | tf_op jit(solution)/shard_map/all_to_all | solution.py:124
  301.3 0.7 copy.128
  302.0 13.2 %all-to-all-done.5 = f32[128,2,128]{2,1,0:T(2,128)S(1)} async-done(((f32[128,2,128]{2,1,0:T(2,128)}), f32[128,2,128]{2,1,0:T(2,128)S(1)}, u32[]{:S(2)}, u32[]{:S(2)}) %all-to-all-start.5) | async-done | bytes 131104 | tf_op jit(solution)/shard_map/all_to_all | solution.py:124
  315.2 5.7 %all-to-all-start.4 = ((f32[128,2,128]{2,1,0:T(2,128)}), f32[128,2,128]{2,1,0:T(2,128)S(1)}, u32[]{:S(2)}, u32[]{:S(2)}) async-start(f32[128,2,128]{2,1,0:T(2,128)} %copy.128), calls=%async_computation.4 | async-start | bytes 262144 | tf_op jit(solution)/shard_map/all_to_all | solution.py:122
  321.8 0.8 copy.120
  322.6 12.3 %all-to-all-done.4 = f32[128,2,128]{2,1,0:T(2,128)S(1)} async-done(((f32[128,2,128]{2,1,0:T(2,128)}), f32[128,2,128]{2,1,0:T(2,128)S(1)}, u32[]{:S(2)}, u32[]{:S(2)}) %all-to-all-start.4) | async-done | bytes 131104 | tf_op jit(solution)/shard_map/all_to_all | solution.py:122
  334.9 5.7 %all-to-all-start.1 = ((f32[128,2,128]{2,1,0:T(2,128)}), f32[128,2,128]{2,1,0:T(2,128)S(1)}, u32[]{:S(2)}, u32[]{:S(2)}) async-start(f32[128,2,128]{2,1,0:T(2,128)} %copy.120), calls=%async_computation.1 | async-start | bytes 262144 | tf_op jit(solution)/shard_map/all_to_all | solution.py:121
  341.0 13.5 %all-to-all-done.1 = f32[128,2,128]{2,1,0:T(2,128)S(1)} async-done(((f32[128,2,128]{2,1,0:T(2,128)}), f32[128,2,128]{2,1,0:T(2,128)S(1)}, u32[]{:S(2)}, u32[]{:S(2)}) %all-to-all-start.1) | async-done | bytes 131104 | tf_op jit(solution)/shard_map/all_to_all | solution.py:121
  360.1 0.7 copy.143
  360.9 5.7 %all-to-all-start.6 = ((f32[2,128,128]{2,0,1:T(2,128)}), f32[2,128,128]{2,0,1:T(2,128)S(1)}, u32[]{:S(2)}, u32[]{:S(2)}) async-start(f32[2,128,128]{2,0,1:T(2,128)} %copy.143), calls=%async_computation.6 | async-start | bytes 262144 | tf_op jit(solution)/shard_map/all_to_all | solution.py:136
  367.3 0.8 copy.149
  368.1 12.5 %all-to-all-done.6 = f32[2,128,128]{2,0,1:T(2,128)S(1)} async-done(((f32[2,128,128]{2,0,1:T(2,128)}), f32[2,128,128]{2,0,1:T(2,128)S(1)}, u32[]{:S(2)}, u32[]{:S(2)}) %all-to-all-start.6) | async-done | bytes 131104 | tf_op jit(solution)/shard_map/all_to_all | solution.py:136
  380.6 5.7 %all-to-all-start.7 = ((f32[2,128,128]{2,0,1:T(2,128)}), f32[2,128,128]{2,0,1:T(2,128)S(1)}, u32[]{:S(2)}, u32[]{:S(2)}) async-start(f32[2,128,128]{2,0,1:T(2,128)} %copy.149), calls=%async_computation.7 | async-start | bytes 262144 | tf_op jit(solution)/shard_map/all_to_all | solution.py:137
  386.5 14.0 %all-to-all-done.7 = f32[2,128,128]{2,0,1:T(2,128)S(1)} async-done(((f32[2,128,128]{2,0,1:T(2,128)}), f32[2,128,128]{2,0,1:T(2,128)S(1)}, u32[]{:S(2)}, u32[]{:S(2)}) %all-to-all-start.7) | async-done | bytes 131104 | tf_op jit(solution)/shard_map/all_to_all | solution.py:137
  402.0 5.7 %all-to-all-start.8 = ((f32[64,2,128]{2,1,0:T(2,128)}), f32[64,2,128]{2,1,0:T(2,128)S(1)}, u32[]{:S(2)}, u32[]{:S(2)}) async-start(f32[64,2,128]{2,1,0:T(2,128)} %copy.152), calls=%async_computation.8 | async-start | bytes 131072 | tf_op jit(solution)/shard_map/all_to_all | solution.py:147
  407.7 54.8 %all-gather.8.cloned.1.call-done = bf16[128,8192]{1,0:T(8,128)(2,1)} async-done(((bf16[128,128]{1,0:T(8,128)(2,1)}), bf16[128,8192]{1,0:T(8,128)(2,1)}) %all-gather.8.cloned.1.call-update) | async-done | bytes 2097168 | tf_op jit(solution)/shard_map/all_gather | solution.py:156
  462.6 4.3 fusion.57
  466.9 52.7 %reduce-scatter.2.cloned.1.call-done = f32[128,1024]{1,0:T(8,128)} async-done(((f32[128,8192]{1,0:T(8,128)}), f32[128,1024]{1,0:T(8,128)}) %reduce-scatter.2.cloned.1.call-update) | async-done | bytes 524304 | tf_op jit(solution)/shard_map/reduce_scatter | solution.py:176
  519.6 1.8 convert_element_type.116
  (63 shorter events, 13.1 us)
Async XLA Ops:
  6.5 50.1 %all-gather.6.cloned.1.call-start = ((), (), s32[]{:S(2)}) async-start(), calls=%async_computation.11 | async-start | bytes 2359296 | tf_op jit(solution)/shard_map/all_gather | solution.py:158
  7.3 232.4 %all-gather.4.cloned.1.call-start = ((), (), s32[]{:S(2)}) async-start(), calls=%async_computation.10 | async-start | bytes 6389760 | tf_op jit(solution)/shard_map/all_gather | solution.py:155
  8.0 244.7 %all-to-all-start.2 = ((f32[1,128,128]{2,0,1:T(1,128)}), f32[1,128,128]{2,0,1:T(1,128)S(1)}, u32[]{:S(2)}, u32[]{:S(2)}) async-start(f32[1,128,128]{2,0,1:T(1,128)} %bitcast.186), calls=%async_computation.2 | async-start | bytes 131072 | tf_op jit(solution)/shard_map/all_to_all | solution.py:99
  244.3 7.6 %collective-permute-start = (bf16[3,2,128]{2,1,0:T(2,128)(2,1)S(1)}, bf16[3,2,128]{2,1,0:T(2,128)(2,1)S(1)}, u32[]{:S(2)}, u32[]{:S(2)}) collective-permute-start(bf16[3,2,128]{2,1,0:T(2,128)(2,1)S(1)} %slice.60), channel_id=1, source_target_pairs={{0,8},{8,16},{16,24},{24,32},{32,40},{40,48},{48,56},{56,64},{64,7... | collective-permute-start | bytes 4616 | tf_op jit(solution)/shard_map/ppermute | solution.py:13
  252.7 21.3 %all-to-all-start = ((f32[1,128,128]{2,0,1:T(1,128)}), f32[1,128,128]{2,0,1:T(1,128)S(1)}, u32[]{:S(2)}, u32[]{:S(2)}) async-start(f32[1,128,128]{2,0,1:T(1,128)} %bitcast.5), calls=%async_computation | async-start | bytes 131072 | tf_op jit(solution)/shard_map/all_to_all | solution.py:98
  276.1 19.5 %all-to-all-start.3 = ((f32[128,2,128]{2,1,0:T(2,128)}), f32[128,2,128]{2,1,0:T(2,128)S(1)}, u32[]{:S(2)}, u32[]{:S(2)}) async-start(f32[128,2,128]{2,1,0:T(2,128)} %copy.124), calls=%async_computation.3 | async-start | bytes 262144 | tf_op jit(solution)/shard_map/all_to_all | solution.py:123
  295.6 19.7 %all-to-all-start.5 = ((f32[128,2,128]{2,1,0:T(2,128)}), f32[128,2,128]{2,1,0:T(2,128)S(1)}, u32[]{:S(2)}, u32[]{:S(2)}) async-start(f32[128,2,128]{2,1,0:T(2,128)} %copy.130), calls=%async_computation.5 | async-start | bytes 262144 | tf_op jit(solution)/shard_map/all_to_all | solution.py:124
  315.2 19.7 %all-to-all-start.4 = ((f32[128,2,128]{2,1,0:T(2,128)}), f32[128,2,128]{2,1,0:T(2,128)S(1)}, u32[]{:S(2)}, u32[]{:S(2)}) async-start(f32[128,2,128]{2,1,0:T(2,128)} %copy.128), calls=%async_computation.4 | async-start | bytes 262144 | tf_op jit(solution)/shard_map/all_to_all | solution.py:122
  321.0 141.6 %all-gather.8.cloned.1.call-start = ((), (), s32[]{:S(2)}) async-start(), calls=%async_computation.12 | async-start | bytes 2129920 | tf_op jit(solution)/shard_map/all_gather | solution.py:156
  334.9 19.7 %all-to-all-start.1 = ((f32[128,2,128]{2,1,0:T(2,128)}), f32[128,2,128]{2,1,0:T(2,128)S(1)}, u32[]{:S(2)}, u32[]{:S(2)}) async-start(f32[128,2,128]{2,1,0:T(2,128)} %copy.120), calls=%async_computation.1 | async-start | bytes 262144 | tf_op jit(solution)/shard_map/all_to_all | solution.py:121
  360.1 102.5 %copy-start = (f32[128]{0:T(128)S(1)}, f32[128]{0:T(128)}, u32[]{:S(2)}) copy-start(f32[128]{0:T(128)} %param.10) | copy-start | bytes 1540
  360.9 19.7 %all-to-all-start.6 = ((f32[2,128,128]{2,0,1:T(2,128)}), f32[2,128,128]{2,0,1:T(2,128)S(1)}, u32[]{:S(2)}, u32[]{:S(2)}) async-start(f32[2,128,128]{2,0,1:T(2,128)} %copy.143), calls=%async_computation.6 | async-start | bytes 262144 | tf_op jit(solution)/shard_map/all_to_all | solution.py:136
  380.6 19.8 %all-to-all-start.7 = ((f32[2,128,128]{2,0,1:T(2,128)}), f32[2,128,128]{2,0,1:T(2,128)S(1)}, u32[]{:S(2)}, u32[]{:S(2)}) async-start(f32[2,128,128]{2,0,1:T(2,128)} %copy.149), calls=%async_computation.7 | async-start | bytes 262144 | tf_op jit(solution)/shard_map/all_to_all | solution.py:137
  402.0 60.6 %all-to-all-start.8 = ((f32[64,2,128]{2,1,0:T(2,128)}), f32[64,2,128]{2,1,0:T(2,128)S(1)}, u32[]{:S(2)}, u32[]{:S(2)}) async-start(f32[64,2,128]{2,1,0:T(2,128)} %copy.152), calls=%async_computation.8 | async-start | bytes 131072 | tf_op jit(solution)/shard_map/all_to_all | solution.py:147
  407.7 111.9 %reduce-scatter.2.cloned.1.call-start = ((), (), s32[]{:S(2)}) async-start(), calls=%async_computation.13 | async-start | bytes 4718592 | tf_op jit(solution)/shard_map/reduce_scatter | solution.py:176
Sparse Core Ops, SparseCore 0:
  9.4 47.1 all-gather.5
  61.0 178.5 all-gather.3
  326.1 136.4 all-gather.7
  467.0 52.4 reduce-scatter.1
where the time goes:
time: 529 us; the launch traced here: 528 us
  waiting for transfers between devices  418 us (79%)
  starting transfers between devices  69.7 us (13%)
  matrix products  17.3 us (3%)
  between operations  13.5 us (3%)
  local copies, waits for them, and re-layouts  6.82 us (1%)
    all_gather x1, waiting for transfers between devices, per_device(): full_in = lax.all_gather(in_proj, 'seq', axis=1, tiled=True)  183 us
    all_gather x1, waiting for transfers between devices, per_device(): full_out = lax.all_gather(out_proj, 'seq', axis=1, tiled=True)  54.8 us
    reduce_scatter x1, waiting for transfers between devices, per_device(): mixed = lax.psum_scatter(terms, 'tp', scatter_dimension=1, tiled=True)  52.7 us
    all_gather x1, waiting for transfers between devices, per_device(): lax.all_gather(part, 'tp', axis=1, tiled=True)  28.7 us
    all_to_all x1, starting transfers between devices, long_convolve(): lax.all_to_all(long_filter[None], 'seq', split_axis=1, concat_axis=0, til...  19.1 us
    all_to_all x1, waiting for transfers between devices, long_convolve(): lax.all_to_all(back_imag, 'seq', split_axis=1, concat_axis=0, tiled=True)  14 us
    all_to_all x1, waiting for transfers between devices, long_convolve(): lax.all_to_all(inner_real, 'seq', split_axis=0, concat_axis=1, tiled=True)  13.5 us
    all_to_all x1, waiting for transfers between devices, long_convolve(): lax.all_to_all(filter_real, 'seq', split_axis=0, concat_axis=1, tiled=True)  13.2 us
  transfers between devices with their start and end apart: 14, of which 12 were waited for; matrix products, arithmetic and copies ran while one was open for 4% of the time, Pallas kernels for 0%

commit v1 on v0

--- a/solution.py
+++ b/solution.py
@@ -152,7 +152,9 @@
     tok_rows = features.shape[0]
     chan_dev = in_proj.shape[2]
     taps_count = short_taps.shape[1]
-    full_in = lax.all_gather(in_proj, "seq", axis=1, tiled=True)
+    full_in = jnp.concatenate(
+        lax.all_to_all(jnp.stack([in_proj] * lax.axis_size("seq")), "seq", 0, 0), axis=1
+    )
     full_out = lax.all_gather(out_proj, "seq", axis=1, tiled=True)
     empty = jnp.zeros((3, tok_rows, chan_dev), jnp.float32)
     piece = jax.tree.map(lambda part: lax.all_gather(part, "tp", axis=1, tiled=True), features)

time: 529 us -> 501 us (0.947)
  waiting for transfers between devices: 418 us -> 356 us
  starting transfers between devices: 69.7 us -> 89.5 us
  local copies, waits for them, and re-layouts: 6.82 us -> 19.2 us
    all_gather x1 -> x0, waiting for transfers between devices: 183 us -> none  [per_device(): full_in = lax.all_gather(in_proj, 'seq', axis=1, tiled=True)]
    all_to_all x0 -> x1, waiting for transfers between devices: none -> 171 us  [per_device(): lax.all_to_all(jnp.stack([in_proj] * lax.axis_size('seq')), 'seq', 0, 0)]
    all_gather x1, waiting for transfers between devices: 28.7 us -> 0.01 us  [per_device(): lax.all_gather(part, 'tp', axis=1, tiled=True)]
    all_to_all x0 -> x1, starting transfers between devices: none -> 19.4 us  [per_device(): lax.all_to_all(jnp.stack([in_proj] * lax.axis_size('seq')), 'seq', 0, 0)]
    all_gather x1, waiting for transfers between devices: 54.8 us -> 35.9 us  [per_device(): full_out = lax.all_gather(out_proj, 'seq', axis=1, tiled=True)]
    reshape x0 -> x1, local copies, waits for them, and re-layouts: none -> 8.05 us  [per_device(): jnp.concatenate(lax.all_to_all(jnp.stack([in_proj] * lax.axis_size('seq')...]
    all_to_all x1, starting transfers between devices: 19.1 us -> 12 us  [long_convolve(): lax.all_to_all(long_filter[None], 'seq', split_axis=1, concat_axis=0, til...]
    all_to_all x1, starting transfers between devices: 7.69 us -> 14.3 us  [long_convolve(): lax.all_to_all(inner[None], 'seq', split_axis=1, concat_axis=0, tiled=True)]
  transfers between devices with their start and end apart: 14 -> 14, of which waited for: 12 -> 11; matrix products, arithmetic and copies ran while one was open for 4% -> 5% of each run, Pallas kernels for 0% -> 0%
where the time goes in v1:
time: 501 us; the launch traced here: 500 us
  waiting for transfers between devices  356 us (71%)
  starting transfers between devices  89.5 us (18%)
  local copies, waits for them, and re-layouts  19.2 us (4%)
  matrix products  17.3 us (3%)
  between operations  15.3 us (3%)
    all_to_all x1, waiting for transfers between devices, per_device(): lax.all_to_all(jnp.stack([in_proj] * lax.axis_size('seq')), 'seq', 0, 0)  171 us
    reduce_scatter x1, waiting for transfers between devices, per_device(): mixed = lax.psum_scatter(terms, 'tp', scatter_dimension=1, tiled=True)  52.7 us
    all_gather x1, waiting for transfers between devices, per_device(): full_out = lax.all_gather(out_proj, 'seq', axis=1, tiled=True)  35.9 us
    all_to_all x1, starting transfers between devices, per_device(): lax.all_to_all(jnp.stack([in_proj] * lax.axis_size('seq')), 'seq', 0, 0)  19.4 us
    all_to_all x1, starting transfers between devices, long_convolve(): lax.all_to_all(inner[None], 'seq', split_axis=1, concat_axis=0, tiled=True)  14.3 us
    all_to_all x1, waiting for transfers between devices, long_convolve(): lax.all_to_all(back_imag, 'seq', split_axis=1, concat_axis=0, tiled=True)  13.8 us
    all_to_all x1, waiting for transfers between devices, long_convolve(): lax.all_to_all(filter_real, 'seq', split_axis=0, concat_axis=1, tiled=True)  13.7 us
    all_to_all x1, waiting for transfers between devices, long_convolve(): lax.all_to_all(inner_imag, 'seq', split_axis=0, concat_axis=1, tiled=True)  13.2 us
  transfers between devices with their start and end apart: 14, of which 11 were waited for; matrix products, arithmetic and copies ran while one was open for 5% of the time, Pallas kernels for 0%

profile of v1, /device:TPU:2, one launch (start us, length us, event | category | flops | bytes accessed | tf_op | source)
XLA Modules:
  0.0 500.5 jit_solution(646098106519660933)
XLA Ops:
  7.4 5.1 %stack.2 = bf16[64,3,128,128]{3,2,1,0:T(8,128)(2,1)} broadcast(bf16[3,128,128]{2,1,0:T(8,128)(2,1)} %param.7), dimensions={1,2,3} | broadcast | bytes 6389760 | tf_op jit(solution)/shard_map/stack | solution.py:156
  12.5 19.4 %all-to-all-start = ((bf16[64,3,128,128]{3,2,1,0:T(8,128)(2,1)}), bf16[64,3,128,128]{3,2,1,0:T(8,128)(2,1)}, u32[]{:S(2)}, u32[]{:S(2)}) async-start(bf16[64,3,128,128]{3,2,1,0:T(8,128)(2,1)} %stack.2), calls=%async_computation | async-start | bytes 12582912 | tf_op jit(solution)/shard_map/all_to_all | solution.py:156
  32.7 170.6 %all-to-all-done = bf16[64,3,128,128]{3,2,1,0:T(8,128)(2,1)} async-done(((bf16[64,3,128,128]{3,2,1,0:T(8,128)(2,1)}), bf16[64,3,128,128]{3,2,1,0:T(8,128)(2,1)}, u32[]{:S(2)}, u32[]{:S(2)}) %all-to-all-start) | async-done | bytes 6291488 | tf_op jit(solution)/shard_map/all_to_all | solution.py:156
  203.2 12.0 %all-to-all-start.3 = ((f32[1,128,128]{2,0,1:T(1,128)}), f32[1,128,128]{2,0,1:T(1,128)S(1)}, u32[]{:S(2)}, u32[]{:S(2)}) async-start(f32[1,128,128]{2,0,1:T(1,128)} %bitcast.13), calls=%async_computation.3 | async-start | bytes 131072 | tf_op jit(solution)/shard_map/all_to_all | solution.py:99
  215.2 8.1 %copy.119 = bf16[3,64,128,128]{3,2,1,0:T(8,128)(2,1)} copy(bf16[3,64,128,128]{3,2,0,1:T(8,128)(2,1)} %bitcast) | data formatting | bytes 12582912 | tf_op jit(solution)/shard_map/reshape | solution.py:155
  223.2 4.7 fusion.11
  227.9 3.4 collective-permute-start
  231.5 4.1 collective-permute-done
  236.3 14.3 %all-to-all-start.1 = ((f32[1,128,128]{2,0,1:T(1,128)}), f32[1,128,128]{2,0,1:T(1,128)S(1)}, u32[]{:S(2)}, u32[]{:S(2)}) async-start(f32[1,128,128]{2,0,1:T(1,128)} %bitcast.7), calls=%async_computation.1 | async-start | bytes 131072 | tf_op jit(solution)/shard_map/all_to_all | solution.py:98
  251.0 13.2 %all-to-all-done.1 = f32[1,128,128]{2,0,1:T(1,128)S(1)} async-done(((f32[1,128,128]{2,0,1:T(1,128)}), f32[1,128,128]{2,0,1:T(1,128)S(1)}, u32[]{:S(2)}, u32[]{:S(2)}) %all-to-all-start.1) | async-done | bytes 65568 | tf_op jit(solution)/shard_map/all_to_all | solution.py:98
  265.6 0.8 copy.131
  266.3 5.5 %all-to-all-start.5 = ((f32[128,2,128]{2,1,0:T(2,128)}), f32[128,2,128]{2,1,0:T(2,128)S(1)}, u32[]{:S(2)}, u32[]{:S(2)}) async-start(f32[128,2,128]{2,1,0:T(2,128)} %copy.131), calls=%async_computation.5 | async-start | bytes 262144 | tf_op jit(solution)/shard_map/all_to_all | solution.py:122
  271.9 0.7 copy.133
  272.6 13.2 %all-to-all-done.5 = f32[128,2,128]{2,1,0:T(2,128)S(1)} async-done(((f32[128,2,128]{2,1,0:T(2,128)}), f32[128,2,128]{2,1,0:T(2,128)S(1)}, u32[]{:S(2)}, u32[]{:S(2)}) %all-to-all-start.5) | async-done | bytes 131104 | tf_op jit(solution)/shard_map/all_to_all | solution.py:122
  285.8 5.7 %all-to-all-start.6 = ((f32[128,2,128]{2,1,0:T(2,128)}), f32[128,2,128]{2,1,0:T(2,128)S(1)}, u32[]{:S(2)}, u32[]{:S(2)}) async-start(f32[128,2,128]{2,1,0:T(2,128)} %copy.133), calls=%async_computation.6 | async-start | bytes 262144 | tf_op jit(solution)/shard_map/all_to_all | solution.py:124
  292.1 0.8 copy.123
  292.9 12.6 %all-to-all-done.6 = f32[128,2,128]{2,1,0:T(2,128)S(1)} async-done(((f32[128,2,128]{2,1,0:T(2,128)}), f32[128,2,128]{2,1,0:T(2,128)S(1)}, u32[]{:S(2)}, u32[]{:S(2)}) %all-to-all-start.6) | async-done | bytes 131104 | tf_op jit(solution)/shard_map/all_to_all | solution.py:124
  305.5 5.7 %all-to-all-start.2 = ((f32[128,2,128]{2,1,0:T(2,128)}), f32[128,2,128]{2,1,0:T(2,128)S(1)}, u32[]{:S(2)}, u32[]{:S(2)}) async-start(f32[128,2,128]{2,1,0:T(2,128)} %copy.123), calls=%async_computation.2 | async-start | bytes 262144 | tf_op jit(solution)/shard_map/all_to_all | solution.py:121
  311.5 0.8 copy.127
  312.3 12.8 %all-to-all-done.2 = f32[128,2,128]{2,1,0:T(2,128)S(1)} async-done(((f32[128,2,128]{2,1,0:T(2,128)}), f32[128,2,128]{2,1,0:T(2,128)S(1)}, u32[]{:S(2)}, u32[]{:S(2)}) %all-to-all-start.2) | async-done | bytes 131104 | tf_op jit(solution)/shard_map/all_to_all | solution.py:121
  325.1 5.7 %all-to-all-start.4 = ((f32[128,2,128]{2,1,0:T(2,128)}), f32[128,2,128]{2,1,0:T(2,128)S(1)}, u32[]{:S(2)}, u32[]{:S(2)}) async-start(f32[128,2,128]{2,1,0:T(2,128)} %copy.127), calls=%async_computation.4 | async-start | bytes 262144 | tf_op jit(solution)/shard_map/all_to_all | solution.py:123
  331.1 13.7 %all-to-all-done.4 = f32[128,2,128]{2,1,0:T(2,128)S(1)} async-done(((f32[128,2,128]{2,1,0:T(2,128)}), f32[128,2,128]{2,1,0:T(2,128)S(1)}, u32[]{:S(2)}, u32[]{:S(2)}) %all-to-all-start.4) | async-done | bytes 131104 | tf_op jit(solution)/shard_map/all_to_all | solution.py:123
  351.1 6.0 %all-to-all-start.7 = ((f32[2,128,128]{2,0,1:T(2,128)}), f32[2,128,128]{2,0,1:T(2,128)S(1)}, u32[]{:S(2)}, u32[]{:S(2)}) async-start(f32[2,128,128]{2,0,1:T(2,128)} %copy.146), calls=%async_computation.7 | async-start | bytes 262144 | tf_op jit(solution)/shard_map/all_to_all | solution.py:136
  357.7 0.8 copy.152
  358.5 12.5 %all-to-all-done.7 = f32[2,128,128]{2,0,1:T(2,128)S(1)} async-done(((f32[2,128,128]{2,0,1:T(2,128)}), f32[2,128,128]{2,0,1:T(2,128)S(1)}, u32[]{:S(2)}, u32[]{:S(2)}) %all-to-all-start.7) | async-done | bytes 131104 | tf_op jit(solution)/shard_map/all_to_all | solution.py:136
  371.0 6.0 %all-to-all-start.8 = ((f32[2,128,128]{2,0,1:T(2,128)}), f32[2,128,128]{2,0,1:T(2,128)S(1)}, u32[]{:S(2)}, u32[]{:S(2)}) async-start(f32[2,128,128]{2,0,1:T(2,128)} %copy.152), calls=%async_computation.8 | async-start | bytes 262144 | tf_op jit(solution)/shard_map/all_to_all | solution.py:137
  377.1 13.8 %all-to-all-done.8 = f32[2,128,128]{2,0,1:T(2,128)S(1)} async-done(((f32[2,128,128]{2,0,1:T(2,128)}), f32[2,128,128]{2,0,1:T(2,128)S(1)}, u32[]{:S(2)}, u32[]{:S(2)}) %all-to-all-start.8) | async-done | bytes 131104 | tf_op jit(solution)/shard_map/all_to_all | solution.py:137
  392.5 5.7 %all-to-all-start.9 = ((f32[64,2,128]{2,1,0:T(2,128)}), f32[64,2,128]{2,1,0:T(2,128)S(1)}, u32[]{:S(2)}, u32[]{:S(2)}) async-start(f32[64,2,128]{2,1,0:T(2,128)} %copy.155), calls=%async_computation.9 | async-start | bytes 131072 | tf_op jit(solution)/shard_map/all_to_all | solution.py:147
  398.3 35.9 %all-gather.5.cloned.1.call-done = bf16[128,8192]{1,0:T(8,128)(2,1)} async-done(((bf16[128,128]{1,0:T(8,128)(2,1)}), bf16[128,8192]{1,0:T(8,128)(2,1)}) %all-gather.5.cloned.1.call-update) | async-done | bytes 2097168 | tf_op jit(solution)/shard_map/all_gather | solution.py:158
  434.2 4.3 fusion.57
  438.6 52.7 %reduce-scatter.2.cloned.1.call-done = f32[128,1024]{1,0:T(8,128)} async-done(((f32[128,8192]{1,0:T(8,128)}), f32[128,1024]{1,0:T(8,128)}) %reduce-scatter.2.cloned.1.call-update) | async-done | bytes 524304 | tf_op jit(solution)/shard_map/reduce_scatter | solution.py:178
  491.3 1.8 convert_element_type.116
  (66 shorter events, 13.0 us)
Async XLA Ops:
  12.5 20.2 %copy-start = (f32[3,3,128]{2,1,0:T(4,128)S(1)}, f32[3,3,128]{2,1,0:T(4,128)}, u32[]{:S(2)}) copy-start(f32[3,3,128]{2,1,0:T(4,128)} %param.8) | copy-start | bytes 13828
  12.5 190.7 %all-to-all-start = ((bf16[64,3,128,128]{3,2,1,0:T(8,128)(2,1)}), bf16[64,3,128,128]{3,2,1,0:T(8,128)(2,1)}, u32[]{:S(2)}, u32[]{:S(2)}) async-start(bf16[64,3,128,128]{3,2,1,0:T(8,128)(2,1)} %stack.2), calls=%async_computation | async-start | bytes 12582912 | tf_op jit(solution)/shard_map/all_to_all | solution.py:156
  31.9 191.4 %all-gather.3.cloned.1.call-start = ((), (), s32[]{:S(2)}) async-start(), calls=%async_computation.11 | async-start | bytes 2359296 | tf_op jit(solution)/shard_map/all_gather | solution.py:160
  203.2 33.0 %all-to-all-start.3 = ((f32[1,128,128]{2,0,1:T(1,128)}), f32[1,128,128]{2,0,1:T(1,128)S(1)}, u32[]{:S(2)}, u32[]{:S(2)}) async-start(f32[1,128,128]{2,0,1:T(1,128)} %bitcast.13), calls=%async_computation.3 | async-start | bytes 131072 | tf_op jit(solution)/shard_map/all_to_all | solution.py:99
  227.9 7.6 %collective-permute-start = (bf16[3,2,128]{2,1,0:T(2,128)(2,1)S(1)}, bf16[3,2,128]{2,1,0:T(2,128)(2,1)S(1)}, u32[]{:S(2)}, u32[]{:S(2)}) collective-permute-start(bf16[3,2,128]{2,1,0:T(2,128)(2,1)S(1)} %slice.60), channel_id=1, source_target_pairs={{0,8},{8,16},{16,24},{24,32},{32,40},{40,48},{48,56},{56,64},{64,7... | collective-permute-start | bytes 4616 | tf_op jit(solution)/shard_map/ppermute | solution.py:13
  236.3 27.9 %all-to-all-start.1 = ((f32[1,128,128]{2,0,1:T(1,128)}), f32[1,128,128]{2,0,1:T(1,128)S(1)}, u32[]{:S(2)}, u32[]{:S(2)}) async-start(f32[1,128,128]{2,0,1:T(1,128)} %bitcast.7), calls=%async_computation.1 | async-start | bytes 131072 | tf_op jit(solution)/shard_map/all_to_all | solution.py:98
  266.3 19.5 %all-to-all-start.5 = ((f32[128,2,128]{2,1,0:T(2,128)}), f32[128,2,128]{2,1,0:T(2,128)S(1)}, u32[]{:S(2)}, u32[]{:S(2)}) async-start(f32[128,2,128]{2,1,0:T(2,128)} %copy.131), calls=%async_computation.5 | async-start | bytes 262144 | tf_op jit(solution)/shard_map/all_to_all | solution.py:122
  285.8 19.7 %all-to-all-start.6 = ((f32[128,2,128]{2,1,0:T(2,128)}), f32[128,2,128]{2,1,0:T(2,128)S(1)}, u32[]{:S(2)}, u32[]{:S(2)}) async-start(f32[128,2,128]{2,1,0:T(2,128)} %copy.133), calls=%async_computation.6 | async-start | bytes 262144 | tf_op jit(solution)/shard_map/all_to_all | solution.py:124
  291.5 142.7 %all-gather.5.cloned.1.call-start = ((), (), s32[]{:S(2)}) async-start(), calls=%async_computation.12 | async-start | bytes 2129920 | tf_op jit(solution)/shard_map/all_gather | solution.py:158
  305.5 19.7 %all-to-all-start.2 = ((f32[128,2,128]{2,1,0:T(2,128)}), f32[128,2,128]{2,1,0:T(2,128)S(1)}, u32[]{:S(2)}, u32[]{:S(2)}) async-start(f32[128,2,128]{2,1,0:T(2,128)} %copy.123), calls=%async_computation.2 | async-start | bytes 262144 | tf_op jit(solution)/shard_map/all_to_all | solution.py:121
  325.1 19.7 %all-to-all-start.4 = ((f32[128,2,128]{2,1,0:T(2,128)}), f32[128,2,128]{2,1,0:T(2,128)S(1)}, u32[]{:S(2)}, u32[]{:S(2)}) async-start(f32[128,2,128]{2,1,0:T(2,128)} %copy.127), calls=%async_computation.4 | async-start | bytes 262144 | tf_op jit(solution)/shard_map/all_to_all | solution.py:123
  347.9 86.3 %copy-start.1 = (f32[128]{0:T(128)S(1)}, f32[128]{0:T(128)}, u32[]{:S(2)}) copy-start(f32[128]{0:T(128)} %param.10) | copy-start | bytes 1540
  351.1 19.9 %all-to-all-start.7 = ((f32[2,128,128]{2,0,1:T(2,128)}), f32[2,128,128]{2,0,1:T(2,128)S(1)}, u32[]{:S(2)}, u32[]{:S(2)}) async-start(f32[2,128,128]{2,0,1:T(2,128)} %copy.146), calls=%async_computation.7 | async-start | bytes 262144 | tf_op jit(solution)/shard_map/all_to_all | solution.py:136
  371.0 19.9 %all-to-all-start.8 = ((f32[2,128,128]{2,0,1:T(2,128)}), f32[2,128,128]{2,0,1:T(2,128)S(1)}, u32[]{:S(2)}, u32[]{:S(2)}) async-start(f32[2,128,128]{2,0,1:T(2,128)} %copy.152), calls=%async_computation.8 | async-start | bytes 262144 | tf_op jit(solution)/shard_map/all_to_all | solution.py:137
  392.5 41.7 %all-to-all-start.9 = ((f32[64,2,128]{2,1,0:T(2,128)}), f32[64,2,128]{2,1,0:T(2,128)S(1)}, u32[]{:S(2)}, u32[]{:S(2)}) async-start(f32[64,2,128]{2,1,0:T(2,128)} %copy.155), calls=%async_computation.9 | async-start | bytes 131072 | tf_op jit(solution)/shard_map/all_to_all | solution.py:147
  398.3 93.0 %reduce-scatter.2.cloned.1.call-start = ((), (), s32[]{:S(2)}) async-start(), calls=%async_computation.13 | async-start | bytes 4718592 | tf_op jit(solution)/shard_map/reduce_scatter | solution.py:178
Sparse Core Ops, SparseCore 0:
  34.8 156.9 all-gather.2
  438.7 52.5 reduce-scatter.1
Sparse Core Ops, SparseCore 1:
  296.3 137.9 all-gather.4
